TPU v7x, 256 devices: a whole 4x4x8 slice. The times are simulated.
256 devices in a mesh: energy: 64 (over x, z_hi, y), space: 4 (over z_lo, core).
Axes of the slice: x: 4, y: 4, z: 8 (z_hi: 4, z_lo: 2; z = z_hi * 2 + z_lo), core: 2. Of those that a mesh axis runs over, the one named last changes fastest.
Arguments:
- g_lesser: bfloat16 [64, 2, 4, 512, 512], P('energy', None, 'space'), may hold values from -6 to 6, as said below
- w_lesser: bfloat16 [64, 2, 4, 512, 512], P('energy', None, 'space'), may hold values from -6 to 6, as said below
- g_retarded: bfloat16 [64, 2, 4, 4, 512, 512], P('energy', None, 'space'), may hold values from -0.1875 to 0.1875
- energy_index: int32 [64], replicated, may hold values from 0 to 63, each once
Outputs:
- sigma_lesser: bfloat16 [64, 2, 4, 512, 512], P('energy', None, 'space')
- delta_green: bfloat16 [64, 2, 4, 512, 512], P('energy', None, 'space')
Inputs may be any that keep to these rules, and one draw needn't show every extreme that they name: `g_lesser`: anti-Hermitian in every diagonal block at every energy: element (j, i) of component 0 is minus element (i, j), of component 1 equal to it. `w_lesser`: anti-Hermitian in every diagonal block at every energy: element (j, i) of component 0 is minus element (i, j), of component 1 equal to it. `energy_index`: each grid point once.
All inputs are finite; a program needn't handle non-finite values.
Results may differ from a plain program's by a relative error of at most 0.013.
Values may be sent and summed in bfloat16 or wider, within the bound.
A program may use at most 128 MiB of HBM per device.

v0:
```python
import math
import jax
import jax.numpy as jnp
from jax import lax
from jax.sharding import PartitionSpec as P


def twiddles(energy_index, per_device, groups):
    grid_size = energy_index.shape[0]
    padded_len = 2 * grid_size
    row_count = 2 * grid_size
    row_ids = lax.iota(jnp.int32, row_count)
    local_energy = row_ids // (2 * groups)
    component = row_ids // groups % 2
    source = row_ids % groups
    stored = source * per_device + local_energy
    grid_point = energy_index[stored]
    frequency = lax.iota(jnp.int32, padded_len)
    forward_phase = frequency[:, None] * grid_point[None, :] % padded_len
    forward_angle = forward_phase.astype(jnp.float32) * (2.0 * math.pi / padded_len)
    cos_fwd = jnp.cos(forward_angle)
    sin_fwd = jnp.sin(forward_angle)
    real_column = (component == 0)[None, :]
    forward = jnp.concatenate(
        [jnp.where(real_column, cos_fwd, sin_fwd), jnp.where(real_column, -sin_fwd, cos_fwd)],
        axis=0,
    )
    shifted = grid_point + grid_size // 2
    backward_phase = shifted[:, None] * frequency[None, :] % padded_len
    backward_angle = backward_phase.astype(jnp.float32) * (2.0 * math.pi / padded_len)
    cos_back = jnp.cos(backward_angle)
    sin_back = jnp.sin(backward_angle)
    real_row = (component == 0)[:, None]
    factor = grid_size ** (-0.5) / padded_len
    left_half = jnp.where(real_row, -sin_back, cos_back) * factor
    right_half = jnp.where(real_row, -cos_back, -sin_back) * factor
    backward = jnp.concatenate([left_half, right_half], axis=1)
    return (forward, backward)


def transform(matrix_high, matrix_low, operand):
    return jnp.dot(matrix_high, operand, preferred_element_type=jnp.float32) + jnp.dot(
        matrix_low, operand, preferred_element_type=jnp.float32
    )


def convolve(green_rows, screen_rows, forward, backward):
    padded_len = forward.shape[0] // 2
    forward_high = forward.astype(jnp.bfloat16)
    forward_low = (forward - forward_high.astype(jnp.float32)).astype(jnp.bfloat16)
    green_hat = transform(forward_high, forward_low, green_rows)
    screen_hat = transform(forward_high, forward_low, screen_rows)
    green_real = green_hat[:padded_len]
    green_imag = green_hat[padded_len:]
    screen_real = screen_hat[:padded_len]
    screen_imag = screen_hat[padded_len:]
    prod_real = green_real * screen_real - green_imag * screen_imag
    prod_imag = green_real * screen_imag + green_imag * screen_real
    merged = jnp.concatenate([prod_real, prod_imag], axis=0)
    return jnp.dot(backward, merged, precision=lax.Precision.HIGH).astype(jnp.bfloat16)


def shards(g_lesser, w_lesser, g_retarded, energy_index):
    energies_here = g_lesser.shape[0]
    width = g_lesser.shape[3]
    groups = lax.axis_size("energy")
    forward, backward = twiddles(energy_index, energies_here, groups)
    own_row = g_retarded[:, :, 0]
    columns = width * width // groups
    green = g_lesser.reshape(energies_here, 2, groups, columns)
    screen = w_lesser.reshape(energies_here, 2, groups, columns)
    green_el, screen_el = (
        lax.all_to_all(green, "energy", split_axis=2, concat_axis=2, tiled=True),
        lax.all_to_all(screen, "energy", split_axis=2, concat_axis=2, tiled=True),
    )
    sigma_el = convolve(
        green_el.reshape(-1, columns), screen_el.reshape(-1, columns), forward, backward
    )
    sigma_el = sigma_el.reshape(energies_here, 2, groups, columns)
    sigma_back = lax.all_to_all(sigma_el, "energy", split_axis=2, concat_axis=2, tiled=True)
    sigma_lesser = sigma_back.reshape(energies_here, 2, 1, width, width)
    first_prod = jnp.einsum(
        "ecnij,ednjl->encdil",
        own_row,
        lax.all_gather(sigma_lesser, "space", axis=2, tiled=True),
        preferred_element_type=jnp.float32,
    )
    left_product = jnp.stack(
        [
            first_prod[:, :, 0, 0] - first_prod[:, :, 1, 1],
            first_prod[:, :, 0, 1] + first_prod[:, :, 1, 0],
        ],
        axis=1,
    ).astype(jnp.bfloat16)
    second_prod = jnp.einsum(
        "ecnil,ednml->ecdim", left_product, own_row, preferred_element_type=jnp.float32
    )
    out_real = second_prod[:, 0, 0] + second_prod[:, 1, 1]
    out_imag = second_prod[:, 1, 0] - second_prod[:, 0, 1]
    delta = jnp.stack([out_real, out_imag], axis=1)
    delta_green = delta.astype(jnp.bfloat16).reshape(energies_here, 2, 1, width, width)
    return (sigma_lesser, delta_green)


def solution(mesh):
    return jax.shard_map(
        shards,
        mesh=mesh,
        in_specs=(
            P("energy", None, "space", None, None),
            P("energy", None, "space", None, None),
            P("energy", None, "space", None, None, None),
            P(),
        ),
        out_specs=(P("energy", None, "space", None, None), P("energy", None, "space", None, None)),
        check_vma=False,
    )
```

profile of v0, /device:TPU:1, one launch (start us, length us, event | category | flops | bytes accessed | tf_op | source)
XLA Modules:
  0.0 215.1 jit_solution(1046797866290290498)
XLA Ops:
  7.2 0.0 copy-start
  7.2 0.0 copy-start.4
  7.2 1.6 reshape.274
  8.8 2.1 copy.28
  10.9 15.1 %all-to-all-start.1 = ((bf16[1,2,64,4096]{3,1,0,2:T(2,128)(2,1)}), bf16[1,2,64,4096]{3,1,0,2:T(2,128)(2,1)S(1)}, u32[]{:S(2)}, u32[]{:S(2)}) async-start(bf16[1,2,64,4096]{3,1,0,2:T(2,128)(2,1)} %copy.28), calls=%async_computation.1 | async-start | bytes 2097152 | tf_op jit(solution)/shard_map/all_to_all | solution.py:74
  26.0 0.0 copy-done.4
  26.0 0.5 reshape.272
  26.6 2.1 copy.26
  28.6 25.1 %all-to-all-done.1 = bf16[1,2,64,4096]{3,1,0,2:T(2,128)(2,1)S(1)} async-done(((bf16[1,2,64,4096]{3,1,0,2:T(2,128)(2,1)}), bf16[1,2,64,4096]{3,1,0,2:T(2,128)(2,1)S(1)}, u32[]{:S(2)}, u32[]{:S(2)}) %all-to-all-start.1) | async-done | bytes 1048608 | tf_op jit(solution)/shard_map/all_to_all | solution.py:74
  53.7 8.3 %all-to-all-start = ((bf16[1,2,64,4096]{3,1,0,2:T(2,128)(2,1)}), bf16[1,2,64,4096]{3,1,0,2:T(2,128)(2,1)S(1)}, u32[]{:S(2)}, u32[]{:S(2)}) async-start(bf16[1,2,64,4096]{3,1,0,2:T(2,128)(2,1)} %copy.26), calls=%async_computation | async-start | bytes 2097152 | tf_op jit(solution)/shard_map/all_to_all | solution.py:73
  62.0 0.2 all-gather.2.cloned.1.call-start
  62.3 0.0 copy-done
  62.3 1.2 gather_fusion
  63.6 0.6 select_multiply_fusion.1
  64.2 0.6 copy.29
  64.8 0.7 fusion.36
  65.5 2.6 %convolution_add_fusion = f32[256,4096]{1,0:T(8,128)} fusion(f32[256,4096]{1,0:T(8,128)S(1)} %fusion.36, bf16[128,4096]{1,0:T(8,128)(2,1)S(1)} %bitcast.74, f32[128,128]{1,0:T(8,128)S(1)} %get-tuple-element.18, f32[128,128]{1,0:T(8,128)S(1)} %get-tuple-element.19), kind=kOutput, calls=%fused_computation.2 | convolution fusion | flops 269647872 | bytes 9568256 | tf_op jit(solution)/shard_map/dot_general | solution.py:42
  68.1 22.7 %all-to-all-done = bf16[1,2,64,4096]{3,1,0,2:T(2,128)(2,1)S(1)} async-done(((bf16[1,2,64,4096]{3,1,0,2:T(2,128)(2,1)}), bf16[1,2,64,4096]{3,1,0,2:T(2,128)(2,1)S(1)}, u32[]{:S(2)}, u32[]{:S(2)}) %all-to-all-start) | async-done | bytes 1048608 | tf_op jit(solution)/shard_map/all_to_all | solution.py:73
  90.8 0.6 copy.27
  91.3 0.7 fusion.38
  92.0 0.0 copy-start.2
  92.0 0.7 convolution_add_fusion.1
  92.8 1.5 copy-done.2
  94.2 0.9 multiply_subtract_fusion
  95.2 1.5 convolution_convert_fusion
  96.7 1.1 copy.30
  97.8 32.1 %all_to_all.15 = bf16[1,2,64,4096]{3,1,0,2:T(2,128)(2,1)S(1)} all-to-all(bf16[1,2,64,4096]{3,1,0,2:T(2,128)(2,1)S(1)} %copy.30), channel_id=1, replica_groups=mesh['energy'=64,'space'=4] {'energy'}, dimensions={2} | all-to-all | bytes 2097152 | tf_op jit(solution)/shard_map/all_to_all | solution.py:80
  130.0 0.6 copy.31
  130.6 1.3 reshape.277
  131.9 0.0 all-gather.2.cloned.1.call-update
  131.9 47.4 %all-gather.2.cloned.1.call-done = bf16[1,2,4,512,512]{4,3,1,0,2:T(8,128)(2,1)} async-done(((bf16[1,2,1,512,512]{4,3,1,0,2:T(8,128)(2,1)}), bf16[1,2,4,512,512]{4,3,1,0,2:T(8,128)(2,1)}) %all-gather.2.cloned.1.call-update) | async-done | bytes 4194320 | tf_op jit(solution)/shard_map/all_gather | solution.py:85
  179.3 14.1 %convolution_bitcast_fusion = f32[1,4,2,2,512,512]{4,5,2,3,1,0:T(8,128)} fusion(bf16[1,2,4,512,512]{4,3,1,0,2:T(8,128)(2,1)} %all-gather.2.cloned.1.call-done, bf16[1,2,1,4,512,512]{5,4,3,2,1,0:T(8,128)(2,1)} %param.6), kind=kOutput, calls=%fused_computation.1 | convolution fusion | flops 4294967296 | bytes 25165824 | tf_op jit(solution)/shard_map/ecnij,ednjl->encdil/dot_general | solution.py:82
  193.4 4.2 %fusion.13 = bf16[1,4,512,512]{2,3,1,0:T(8,128)(2,1)S(1)} fusion(f32[1,4,2,2,512,512]{4,5,2,3,1,0:T(8,128)} %convolution_bitcast_fusion), kind=kLoop, calls=%fused_computation.22 | loop fusion | flops 2097152 | bytes 10485760 | tf_op jit(solution)/shard_map/add | solution.py:91
  197.6 0.0 copy-start.3
  197.6 4.4 %fusion.12 = bf16[1,4,512,512]{2,3,1,0:T(8,128)(2,1)S(1)} fusion(f32[1,4,2,2,512,512]{4,5,2,3,1,0:T(8,128)} %convolution_bitcast_fusion), kind=kLoop, calls=%fused_computation.21 | loop fusion | flops 2097152 | bytes 10485760 | tf_op jit(solution)/shard_map/sub | solution.py:90
  202.1 0.2 copy-done.3
  202.3 0.0 copy-start.1
  202.3 4.5 %fusion.11 = f32[1,2,2,512,512]{4,3,2,1,0:T(8,128)S(1)} fusion(bf16[1,4,512,512]{2,3,1,0:T(8,128)(2,1)S(1)} %fusion.13, bf16[1,4,512,512]{2,3,1,0:T(8,128)(2,1)S(1)} %fusion.12, bf16[1,2,1,4,512,512]{5,4,3,2,1,0:T(8,128)(2,1)S(1)} %copy-done.3), kind=kOutput, calls=%fused_computation.20 | convolution fusion | flops 4303355904 | bytes 12582912 | tf_op jit(solution)/shard_map/ecnil,ednml->ecdim/dot_general | solution.py:95
  206.8 0.4 fusion.15
  207.2 1.1 pad_maximum_fusion
  208.2 0.0 copy-done.1
  (4 shorter events, 0.0 us)
Async XLA Ops:
  7.2 55.1 %copy-start = (s32[64]{0:T(128)S(1)}, s32[64]{0:T(128)}, u32[]{:S(2)}) copy-start(s32[64]{0:T(128)} %param.7) | copy-start | bytes 772
  7.2 18.8 %copy-start.4 = (bf16[1,2,1,512,512]{4,3,2,1,0:T(8,128)(2,1)S(1)}, bf16[1,2,1,512,512]{4,3,2,1,0:T(8,128)(2,1)}, u32[]{:S(2)}) copy-start(bf16[1,2,1,512,512]{4,3,2,1,0:T(8,128)(2,1)} %param.4) | copy-start | bytes 3145732
  10.9 42.8 %all-to-all-start.1 = ((bf16[1,2,64,4096]{3,1,0,2:T(2,128)(2,1)}), bf16[1,2,64,4096]{3,1,0,2:T(2,128)(2,1)S(1)}, u32[]{:S(2)}, u32[]{:S(2)}) async-start(bf16[1,2,64,4096]{3,1,0,2:T(2,128)(2,1)} %copy.28), calls=%async_computation.1 | async-start | bytes 2097152 | tf_op jit(solution)/shard_map/all_to_all | solution.py:74
  53.7 37.0 %all-to-all-start = ((bf16[1,2,64,4096]{3,1,0,2:T(2,128)(2,1)}), bf16[1,2,64,4096]{3,1,0,2:T(2,128)(2,1)S(1)}, u32[]{:S(2)}, u32[]{:S(2)}) async-start(bf16[1,2,64,4096]{3,1,0,2:T(2,128)(2,1)} %copy.26), calls=%async_computation | async-start | bytes 2097152 | tf_op jit(solution)/shard_map/all_to_all | solution.py:73
  62.0 117.3 %all-gather.2.cloned.1.call-start = ((), (), s32[]{:S(2)}) async-start(), calls=%async_computation.3 | async-start | bytes 5242880 | tf_op jit(solution)/shard_map/all_gather | solution.py:85
  92.0 2.2 %copy-start.2 = (f32[256,4096]{1,0:T(8,128)S(1)}, f32[256,4096]{1,0:T(8,128)}, u32[]{:S(2)}) copy-start(f32[256,4096]{1,0:T(8,128)} %convolution_add_fusion) | copy-start | bytes 12582916
  197.6 4.6 %copy-start.3 = (bf16[1,2,1,4,512,512]{5,4,3,2,1,0:T(8,128)(2,1)S(1)}, bf16[1,2,1,4,512,512]{5,4,3,2,1,0:T(8,128)(2,1)}, u32[]{:S(2)}) copy-start(bf16[1,2,1,4,512,512]{5,4,3,2,1,0:T(8,128)(2,1)} %param.6) | copy-start | bytes 12582916
  202.3 6.0 %copy-start.1 = (s32[64]{0:T(128)S(1)}, s32[64]{0:T(128)}, u32[]{:S(2)}) copy-start(s32[64]{0:T(128)} %param.7) | copy-start | bytes 772
Sparse Core Ops, SparseCore 0:
  132.0 47.2 all-gather.1
where the time goes:
time: 215 us
  waiting for transfers between devices  95.2 us (44%)
  blocking collectives  32.1 us (15%)
  matrix products  24.9 us (12%)
  starting transfers between devices  23.7 us (11%)
  between operations  14.2 us (7%)
  local copies, waits for them, and re-layouts  13.4 us (6%)
  other arithmetic  11.6 us (5%)
    all_gather x1, waiting for transfers between devices, shards(): lax.all_gather(sigma_lesser, 'space', axis=2, tiled=True)  47.4 us
    all_to_all x1, blocking collectives, shards(): lax.all_to_all(sigma_el, 'energy', split_axis=2, concat_axis=2, tiled=True)  32.1 us
    all_to_all x1, waiting for transfers between devices, shards(): lax.all_to_all(screen, 'energy', split_axis=2, concat_axis=2, tiled=True)  25.1 us
    all_to_all x1, waiting for transfers between devices, shards(): lax.all_to_all(green, 'energy', split_axis=2, concat_axis=2, tiled=True)  22.7 us
    all_to_all x1, starting transfers between devices, shards(): lax.all_to_all(screen, 'energy', split_axis=2, concat_axis=2, tiled=True)  15.1 us
    dot_general x1, matrix products, shards(): jnp.einsum('ecnij,ednjl->encdil', own_row, lax.all_gather(sigma_lesser, '...  14.1 us
    all_to_all x1, starting transfers between devices, shards(): lax.all_to_all(green, 'energy', split_axis=2, concat_axis=2, tiled=True)  8.33 us
    dot_general x1, matrix products, shards(): jnp.einsum('ecnil,ednml->ecdim', left_product, own_row, preferred_element...  4.54 us
  transfers between devices with their start and end apart: 3, of which 3 were waited for; matrix products, arithmetic and copies ran while one was open for 4% of the time, Pallas kernels for 0%

commit v1 on v0

--- a/solution.py
+++ b/solution.py
@@ -69,8 +69,17 @@
     columns = width * width // groups
     green = g_lesser.reshape(energies_here, 2, groups, columns)
     screen = w_lesser.reshape(energies_here, 2, groups, columns)
+    set_boxes = lambda x_part: jnp.concatenate(
+        jax.lax.all_to_all(
+            jnp.stack(jnp.split(x_part, jax.lax.axis_size("energy"), axis=2), axis=0),
+            axis_name="energy",
+            split_axis=0,
+            concat_axis=0,
+        ),
+        axis=2,
+    )
     green_el, screen_el = (
-        lax.all_to_all(green, "energy", split_axis=2, concat_axis=2, tiled=True),
+        set_boxes(green),
         lax.all_to_all(screen, "energy", split_axis=2, concat_axis=2, tiled=True),
     )
     sigma_el = convolve(

time: 215 us -> 265 us (1.23)
  local copies, waits for them, and re-layouts: 13.4 us -> 58.7 us
  waiting for transfers between devices: 95.2 us -> 98.3 us
    unnamed x10 -> x69, local copies, waits for them, and re-layouts: 1.71 us -> 39.8 us
    all_to_all x1, starting transfers between devices: 8.33 us -> 15.1 us  [shards(): jax.lax.all_to_all(jnp.stack(jnp.split(x_part, jax.lax.axis_size('energy'...]
    all_to_all x1, starting transfers between devices: 15.1 us -> 8.33 us  [shards(): lax.all_to_all(screen, 'energy', split_axis=2, concat_axis=2, tiled=True)]
    add x1 -> x0, other arithmetic: 4.19 us -> none  [shards(): first_prod[:, :, 0, 1] + first_prod[:, :, 1, 0]]
    sub x0 -> x1, local copies, waits for them, and re-layouts: none -> 4.15 us  [shards(): first_prod[:, :, 0, 0] - first_prod[:, :, 1, 1]]
    sub x1, other arithmetic: 4.42 us -> 8 us  [shards(): first_prod[:, :, 0, 0] - first_prod[:, :, 1, 1]]
    dot_general x1, matrix products: 4.54 us -> 7.68 us  [shards(): jnp.einsum('ecnil,ednml->ecdim', left_product, own_row, preferred_element...]
  transfers between devices with their start and end apart: 3 -> 3, of which waited for: 3 -> 3; matrix products, arithmetic and copies ran while one was open for 4% -> 2% of each run, Pallas kernels for 0% -> 0%
where the time goes in v1:
time: 265 us; the launch traced here: 264 us
  waiting for transfers between devices  98.3 us (37%)
  local copies, waits for them, and re-layouts  58.7 us (22%)
  blocking collectives  32.5 us (12%)
  matrix products  26.1 us (10%)
  starting transfers between devices  23.7 us (9%)
  between operations  14.3 us (5%)
  other arithmetic  11 us (4%)
    all_gather x1, waiting for transfers between devices, shards(): lax.all_gather(sigma_lesser, 'space', axis=2, tiled=True)  47.2 us
    unnamed x69, local copies, waits for them, and re-layouts  39.8 us
    all_to_all x1, blocking collectives, shards(): lax.all_to_all(sigma_el, 'energy', split_axis=2, concat_axis=2, tiled=True)  32.5 us
    all_to_all x1, waiting for transfers between devices, shards(): lax.all_to_all(screen, 'energy', split_axis=2, concat_axis=2, tiled=True)  26 us
    all_to_all x1, waiting for transfers between devices, shards(): jax.lax.all_to_all(jnp.stack(jnp.split(x_part, jax.lax.axis_size('energy'...  25.1 us
    all_to_all x1, starting transfers between devices, shards(): jax.lax.all_to_all(jnp.stack(jnp.split(x_part, jax.lax.axis_size('energy'...  15.1 us
    dot_general x1, matrix products, shards(): jnp.einsum('ecnij,ednjl->encdil', own_row, lax.all_gather(sigma_lesser, '...  14.1 us
    all_to_all x1, starting transfers between devices, shards(): lax.all_to_all(screen, 'energy', split_axis=2, concat_axis=2, tiled=True)  8.33 us
  transfers between devices with their start and end apart: 3, of which 3 were waited for; matrix products, arithmetic and copies ran while one was open for 2% of the time, Pallas kernels for 0%

profile of v1, /device:TPU:1, one launch (start us, length us, event | category | flops | bytes accessed | tf_op | source)
XLA Modules:
  0.0 264.5 jit_solution(10439636351570674599)
XLA Ops:
  7.2 1.6 reshape.272
  9.0 0.7 fusion.50
  9.7 0.7 fusion.48
  10.9 0.6 constant_dynamic-update-slice_fusion.63
  11.6 0.6 constant_dynamic-update-slice_fusion.62
  12.2 0.6 constant_dynamic-update-slice_fusion.61
  12.8 0.6 constant_dynamic-update-slice_fusion.60
  13.5 0.6 constant_dynamic-update-slice_fusion.59
  14.1 0.6 constant_dynamic-update-slice_fusion.58
  14.7 0.6 constant_dynamic-update-slice_fusion.57
  15.4 0.6 constant_dynamic-update-slice_fusion.56
  16.6 0.6 constant_dynamic-update-slice_fusion.54
  17.3 0.6 constant_dynamic-update-slice_fusion.53
  17.9 0.6 constant_dynamic-update-slice_fusion.52
  18.5 0.6 constant_dynamic-update-slice_fusion.51
  19.2 0.6 constant_dynamic-update-slice_fusion.50
  19.8 0.6 constant_dynamic-update-slice_fusion.49
  20.4 0.6 constant_dynamic-update-slice_fusion.48
  21.1 0.6 constant_dynamic-update-slice_fusion.47
  21.7 0.6 constant_dynamic-update-slice_fusion.46
  22.3 0.6 constant_dynamic-update-slice_fusion.45
  22.9 0.6 constant_dynamic-update-slice_fusion.44
  23.6 0.6 constant_dynamic-update-slice_fusion.43
  24.2 0.6 constant_dynamic-update-slice_fusion.42
  24.8 0.6 constant_dynamic-update-slice_fusion.41
  25.5 0.6 constant_dynamic-update-slice_fusion.40
  51.4 15.1 %all-to-all-start = ((bf16[64,1,2,1,4096]{4,2,3,1,0:T(2,128)(2,1)}), bf16[64,1,2,1,4096]{4,2,3,1,0:T(2,128)(2,1)S(1)}, u32[]{:S(2)}, u32[]{:S(2)}) async-start(bf16[64,1,2,1,4096]{4,2,3,1,0:T(2,128)(2,1)} %constant_dynamic-update-slice_fusion), calls=%async_computation | async-start | bytes 2097152 | tf_op jit(solution)/shard_map/all_to_all | solution.py:73
  67.0 2.1 copy.1683
  69.1 25.1 %all-to-all-done = bf16[64,1,2,1,4096]{4,2,3,1,0:T(2,128)(2,1)S(1)} async-done(((bf16[64,1,2,1,4096]{4,2,3,1,0:T(2,128)(2,1)}), bf16[64,1,2,1,4096]{4,2,3,1,0:T(2,128)(2,1)S(1)}, u32[]{:S(2)}, u32[]{:S(2)}) %all-to-all-start) | async-done | bytes 1048608 | tf_op jit(solution)/shard_map/all_to_all | solution.py:73
  94.2 8.3 %all-to-all-start.1 = ((bf16[1,2,64,4096]{3,1,0,2:T(2,128)(2,1)}), bf16[1,2,64,4096]{3,1,0,2:T(2,128)(2,1)S(1)}, u32[]{:S(2)}, u32[]{:S(2)}) async-start(bf16[1,2,64,4096]{3,1,0,2:T(2,128)(2,1)} %copy.1683), calls=%async_computation.1 | async-start | bytes 2097152 | tf_op jit(solution)/shard_map/all_to_all | solution.py:83
  102.8 1.2 gather_fusion
  105.2 26.0 %all-to-all-done.1 = bf16[1,2,64,4096]{3,1,0,2:T(2,128)(2,1)S(1)} async-done(((bf16[1,2,64,4096]{3,1,0,2:T(2,128)(2,1)}), bf16[1,2,64,4096]{3,1,0,2:T(2,128)(2,1)S(1)}, u32[]{:S(2)}, u32[]{:S(2)}) %all-to-all-start.1) | async-done | bytes 1048608 | tf_op jit(solution)/shard_map/all_to_all | solution.py:83
  131.8 0.7 fusion.35
  132.5 0.7 convolution_add_fusion
  133.2 0.7 fusion.37
  133.9 0.7 convolution_add_fusion.1
  134.7 0.9 multiply_subtract_fusion
  135.6 1.5 convolution_convert_fusion
  137.2 1.1 copy.1685
  138.3 32.5 %all_to_all.15 = bf16[1,2,64,4096]{3,1,0,2:T(2,128)(2,1)S(1)} all-to-all(bf16[1,2,64,4096]{3,1,0,2:T(2,128)(2,1)S(1)} %copy.1685), channel_id=1, replica_groups=mesh['energy'=64,'space'=4] {'energy'}, dimensions={2} | all-to-all | bytes 2097152 | tf_op jit(solution)/shard_map/all_to_all | solution.py:89
  171.3 1.3 reshape.277
  172.7 47.2 %all-gather.2.cloned.1.call-done = bf16[1,2,4,512,512]{4,3,1,0,2:T(8,128)(2,1)} async-done(((bf16[1,2,1,512,512]{4,3,1,0,2:T(8,128)(2,1)}), bf16[1,2,4,512,512]{4,3,1,0,2:T(8,128)(2,1)}) %all-gather.2.cloned.1.call-update) | async-done | bytes 4194320 | tf_op jit(solution)/shard_map/all_gather | solution.py:94
  219.8 14.1 %convolution_bitcast_fusion = f32[1,4,2,2,512,512]{4,5,2,3,1,0:T(8,128)} fusion(bf16[1,2,4,512,512]{4,3,1,0,2:T(8,128)(2,1)} %all-gather.2.cloned.1.call-done, bf16[1,2,1,4,512,512]{5,4,3,2,1,0:T(8,128)(2,1)} %param.6), kind=kOutput, calls=%fused_computation.1 | convolution fusion | flops 4294967296 | bytes 25165824 | tf_op jit(solution)/shard_map/ecnij,ednjl->encdil/dot_general | solution.py:91
  233.9 8.0 %fusion.11 = (bf16[1,4,512,512]{2,3,1,0:T(8,128)(2,1)}, bf16[1,4,512,512]{2,3,1,0:T(8,128)(2,1)S(1)}) fusion(f32[1,4,2,2,512,512]{4,5,2,3,1,0:T(8,128)} %convolution_bitcast_fusion), kind=kLoop, calls=%fused_computation.19 | loop fusion | flops 4194304 | bytes 20971520 | tf_op jit(solution)/shard_map/sub | solution.py:99
  241.9 4.2 %copy.1690 = bf16[1,4,512,512]{3,2,1,0:T(8,128)(2,1)} copy(bf16[1,4,512,512]{2,3,1,0:T(8,128)(2,1)} %get-tuple-element.68) | data formatting | bytes 4194304 | tf_op jit(solution)/shard_map/sub | solution.py:99
  246.1 2.4 copy.1691
  248.5 7.7 %fusion.10 = f32[1,2,2,512,512]{4,3,2,1,0:T(8,128)S(1)} fusion(bf16[1,4,512,512]{3,2,1,0:T(8,128)(2,1)} %copy.1691, bf16[1,4,512,512]{3,2,1,0:T(8,128)(2,1)} %copy.1690, bf16[1,2,1,4,512,512]{5,4,3,2,1,0:T(8,128)(2,1)} %param.6), kind=kOutput, calls=%fused_computation.18 | convolution fusion | flops 4303355904 | bytes 12582912 | tf_op jit(solution)/shard_map/ecnil,ednml->ecdim/dot_general | solution.py:104
  256.5 1.1 pad_maximum_fusion
  (61 shorter events, 30.2 us)
Async XLA Ops:
  7.2 95.6 %copy-start = (s32[64]{0:T(128)S(1)}, s32[64]{0:T(128)}, u32[]{:S(2)}) copy-start(s32[64]{0:T(128)} %param.7) | copy-start | bytes 772
  9.6 56.9 %copy-start.2 = (bf16[1,2,1,512,512]{4,3,2,1,0:T(8,128)(2,1)S(1)}, bf16[1,2,1,512,512]{4,3,2,1,0:T(8,128)(2,1)}, u32[]{:S(2)}) copy-start(bf16[1,2,1,512,512]{4,3,2,1,0:T(8,128)(2,1)} %param.5) | copy-start | bytes 3145732
  51.4 42.8 %all-to-all-start = ((bf16[64,1,2,1,4096]{4,2,3,1,0:T(2,128)(2,1)}), bf16[64,1,2,1,4096]{4,2,3,1,0:T(2,128)(2,1)S(1)}, u32[]{:S(2)}, u32[]{:S(2)}) async-start(bf16[64,1,2,1,4096]{4,2,3,1,0:T(2,128)(2,1)} %constant_dynamic-update-slice_fusion), calls=%async_computation | async-start | bytes 2097152 | tf_op jit(solution)/shard_map/all_to_all | solution.py:73
  94.2 37.0 %all-to-all-start.1 = ((bf16[1,2,64,4096]{3,1,0,2:T(2,128)(2,1)}), bf16[1,2,64,4096]{3,1,0,2:T(2,128)(2,1)S(1)}, u32[]{:S(2)}, u32[]{:S(2)}) async-start(bf16[1,2,64,4096]{3,1,0,2:T(2,128)(2,1)} %copy.1683), calls=%async_computation.1 | async-start | bytes 2097152 | tf_op jit(solution)/shard_map/all_to_all | solution.py:83
  102.5 117.3 %all-gather.2.cloned.1.call-start = ((), (), s32[]{:S(2)}) async-start(), calls=%async_computation.3 | async-start | bytes 5242880 | tf_op jit(solution)/shard_map/all_gather | solution.py:94
  248.5 9.1 %copy-start.1 = (s32[64]{0:T(128)S(1)}, s32[64]{0:T(128)}, u32[]{:S(2)}) copy-start(s32[64]{0:T(128)} %param.7) | copy-start | bytes 772
Sparse Core Ops, SparseCore 0:
  172.8 47.0 all-gather.1
